TPU v7x, 32 devices: a whole 2x2x4 slice. The times are simulated.
32 devices in a mesh: gx: 2 (over x), gz: 4 (over y, core), ta: 4 (over z).
Axes of the slice: x: 2, y: 2, z: 4, core: 2. Of those that a mesh axis runs over, the one named last changes fastest.
Arguments:
- velocity: bfloat16 [3, 32, 64, 4096], P(None, 'ta', 'gx', 'gz'), may hold values from -6 to 6
- offsets: int32 [7], replicated, may hold values from 0 to 16, as said below
- owner: int32 [7], replicated, may hold values from 0 to 7, as said below
Outputs:
- cross_spectra: float32 [4, 2, 7, 64, 4096], P(None, None, None, 'gx', ('gz', 'ta'))
Inputs may be any that keep to these rules, and one draw needn't show every extreme that they name: `offsets`: each segment of 16 snapshots lies inside the window. owner o names the block of streamwise index o // 4 and spanwise index o mod 4.
All inputs are finite; a program needn't handle non-finite values.
Results may differ from a plain program's by a relative error of at most 0.0062.
Values may be sent and summed in bfloat16 or wider, within the bound.
No kernel may reach another device: no remote copies, remote signals or barrier semaphores. Data moves between devices by JAX's collectives and lax.ppermute only.
A program may use at most 64 MiB of HBM per device.

v0:
```python
import math
import jax
import jax.numpy as jnp
from jax import lax
from jax.sharding import PartitionSpec as P

SEG = 16
NSEG = 7
F = 7


def from_root(shard, axis, root):
    mine = lax.axis_index(axis) == root
    return lax.psum(jnp.where(mine, shard, jnp.zeros_like(shard)), axis)


def padded_2(shard, sides, width):
    for axis, dim in sides:
        devices, length = (lax.axis_size(axis), shard.shape[dim])
        up = [(i, (i + 1) % devices) for i in range(devices)]
        down = [(j, i) for i, j in up]
        last = lax.slice_in_dim(shard, length - width, length, axis=dim)
        first = lax.slice_in_dim(shard, 0, width, axis=dim)
        before = lax.ppermute(last, axis, up)
        after = lax.ppermute(first, axis, down)
        shard = jnp.concatenate([before, shard, after], axis=dim)
    return shard


def dft_table(offsets, step_count_total):
    sample_times = jnp.arange(step_count_total, dtype=jnp.int32)
    temporal_delay = sample_times[None, :] - offsets[:, None]
    inside = (temporal_delay >= 0) & (temporal_delay < SEG)
    window = 0.5 - 0.5 * jnp.cos(2.0 * math.pi / SEG * temporal_delay.astype(jnp.float32))
    frequency = jnp.arange(1, F + 1, dtype=jnp.int32)
    turns = frequency[None, :, None] * temporal_delay[:, None, :] % SEG
    phase_angle = 2.0 * math.pi / SEG * turns.astype(jnp.float32)
    weight = jnp.where(inside, window, jnp.float32(0.0))[:, None, :]
    rows = jnp.stack([weight * jnp.cos(phase_angle), -weight * jnp.sin(phase_angle)], axis=1)
    return rows.reshape(offsets.shape[0] * 2 * F, step_count_total).astype(jnp.bfloat16)


def fourth_order(padded, which_axis, length_cells):

    def shifted(first):
        return lax.slice_in_dim(padded, first, first + length_cells, axis=which_axis)

    return (8.0 * (shifted(3) - shifted(1)) - (shifted(4) - shifted(0))) / 12.0


def spread_series(block_data, root_index):
    return from_root(block_data, ("gx", "gz"), root_index)


def shards(velocity, offsets, owner):
    block_rows = velocity.shape[2]
    block_cols = velocity.shape[3]
    stream_span = jnp.stack([velocity[0], velocity[2]])
    padded = padded_2(stream_span, (("gx", 2), ("gz", 3)), 2).astype(jnp.float32)
    streamwise = padded[0, :, 2 : 2 + block_rows, :]
    spanwise = padded[1, :, :, 2 : 2 + block_cols]
    vorticity = (
        fourth_order(streamwise, 2, block_cols) - fourth_order(spanwise, 1, block_rows)
    ).astype(jnp.bfloat16)
    fields = jnp.concatenate([velocity, vorticity[None]], axis=0)
    step_count_total = velocity.shape[1] * lax.axis_size("ta")
    segment_rows = dft_table(offsets, step_count_total)
    series = lax.all_to_all(fields, "ta", split_axis=3, concat_axis=1, tiled=True)
    flat_series = series.reshape(series.shape[0], series.shape[1], -1)
    power_spectra = jnp.einsum(
        "rt,qtn->qrn", segment_rows, flat_series, preferred_element_type=jnp.float32
    )
    flat_series, power_spectra = (flat_series, power_spectra)
    quantities = flat_series.shape[0]
    cells_here = flat_series.shape[2]
    slab_cols = cells_here // block_rows
    window_rows = dft_table(jnp.zeros((1,), jnp.int32), SEG)
    cospectrum = jnp.zeros((quantities, F, cells_here), jnp.float32)
    quadrature_spectrum = jnp.zeros((quantities, F, cells_here), jnp.float32)
    for segment in range(NSEG):
        local_spec = power_spectra[:, segment * 2 * F : (segment + 1) * 2 * F, :]
        window_piece = lax.dynamic_slice_in_dim(flat_series, offsets[segment], SEG, 1)
        arrived = spread_series(window_piece, owner[segment])
        remote = jnp.einsum("rt,qtn->qrn", window_rows, arrived, preferred_element_type=jnp.float32)
        remote_cos = remote[:, :F]
        remote_sin = remote[:, F:]
        cosine_part_here = local_spec[:, :F]
        local_sin = local_spec[:, F:]
        cospectrum = cospectrum + (remote_cos * cosine_part_here + remote_sin * local_sin)
        quadrature_spectrum = quadrature_spectrum + (
            remote_cos * local_sin - remote_sin * cosine_part_here
        )
    scaling = 8.0 / (3.0 * SEG * NSEG)
    result = jnp.stack([cospectrum, quadrature_spectrum], axis=1) * scaling
    return result.reshape(quantities, 2, F, block_rows, slab_cols)


def solution(mesh):
    in_specs = (P(None, "ta", "gx", "gz"), P(), P())
    out_specs = P(None, None, None, "gx", ("gz", "ta"))
    return jax.shard_map(shards, mesh=mesh, in_specs=in_specs, out_specs=out_specs, check_vma=False)
```

profile of v0, /device:TPU:0, one launch (start us, length us, event | category | flops | bytes accessed | tf_op | source)
XLA Modules:
  0.0 293.2 jit_solution(14867775583435725023)
XLA Ops:
  8.1 3.0 %collective-permute-start = (bf16[2,8,2,1024]{3,1,2,0:T(8,128)(2,1)S(1)}, bf16[2,8,2,1024]{3,1,2,0:T(8,128)(2,1)S(1)}, u32[]{:S(2)}, u32[]{:S(2)}) collective-permute-start(bf16[2,8,2,1024]{3,1,2,0:T(8,128)(2,1)S(1)} %copy.47), channel_id=1, source_target_pairs={{0,16},{16,0},{1,17},{17,1},{2,18},{18,2},{3,19},{19,3},{4,20},{20... | collective-permute-start | bytes 196616 | tf_op jit(solution)/shard_map/ppermute | solution.py:24
  11.2 2.2 collective-permute-done
  15.7 1.7 collective-permute-start.3
  17.4 6.1 %copy.34 = bf16[3,8,32,1024]{2,1,0,3:T(8,128)(2,1)} copy(bf16[3,8,32,1024]{3,2,1,0:T(8,128)(2,1)S(1)} %copy-done) | data formatting | bytes 3145728 | tf_op args[0]
  24.8 4.7 %copy.33 = bf16[2,8,36,1028]{2,1,3,0:T(8,128)(2,1)} copy(bf16[2,8,36,1028]{3,1,2,0:T(8,128)(2,1)S(1)} %concatenate.11) | data formatting | bytes 2368512 | tf_op jit(solution)/shard_map/concatenate | solution.py:26
  29.5 2.5 convert_element_type.78
  33.6 4.4 %fusion.8 = bf16[1,8,32,1024]{2,1,0,3:T(8,128)(2,1)} fusion(f32[8,36,1024]{1,0,2:T(8,128)S(1)} %slice_bitcast_fusion.1, f32[8,32,1028]{1,0,2:T(8,128)S(1)} %slice_bitcast_fusion), kind=kLoop, calls=%fused_computation.23 | loop fusion | flops 3145728 | bytes 8912896 | tf_op jit(solution)/shard_map/broadcast_in_dim | solution.py:65
  38.1 6.7 %fusion.33 = bf16[1024,4,8,32]{3,2,1,0:T(8,128)(2,1)} fusion(bf16[1,8,32,1024]{2,1,0,3:T(8,128)(2,1)} %fusion.8, bf16[3,8,32,1024]{2,1,0,3:T(8,128)(2,1)S(1)} %bitcast.65), kind=kLoop, calls=%fused_computation.82 | loop fusion | flops 1048576 | bytes 4194304
  44.8 10.6 %reshape.340 = bf16[4,2,131072]{2,1,0:T(2,128)(2,1)} reshape(bf16[1024,4,8,32]{3,2,1,0:T(8,128)(2,1)} %fusion.33) | data formatting | bytes 4194304
  55.4 5.0 %all-to-all-start = ((bf16[4,2,131072]{2,1,0:T(2,128)(2,1)}), bf16[4,2,131072]{2,1,0:T(2,128)(2,1)S(1)}, u32[]{:S(2)}, u32[]{:S(2)}) async-start(bf16[4,2,131072]{2,1,0:T(2,128)(2,1)} %reshape.340), calls=%async_computation | async-start | bytes 4194304 | tf_op jit(solution)/shard_map/all_to_all | solution.py:68
  79.1 29.5 %all-to-all-done = bf16[4,2,131072]{2,1,0:T(2,128)(2,1)S(1)} async-done(((bf16[4,2,131072]{2,1,0:T(2,128)(2,1)}), bf16[4,2,131072]{2,1,0:T(2,128)(2,1)S(1)}, u32[]{:S(2)}, u32[]{:S(2)}) %all-to-all-start) | async-done | bytes 2097184 | tf_op jit(solution)/shard_map/all_to_all | solution.py:68
  108.6 5.6 %reshape.341 = bf16[1024,4,8,32]{3,2,1,0:T(8,128)(2,1)} reshape(bf16[4,2,131072]{2,1,0:T(2,128)(2,1)S(1)} %all-to-all-done) | data formatting | bytes 4194304
  114.3 8.8 %copy.35 = bf16[4,8,32,4,256]{4,1,2,3,0:T(8,128)(2,1)S(1)} copy(bf16[4,8,32,4,256]{2,1,0,4,3:T(8,128)(2,1)} %bitcast.63) | data formatting | bytes 4194304 | tf_op jit(solution)/shard_map/all_to_all | solution.py:68
  123.1 4.5 %dynamic-slice_select_fusion.6 = (bf16[4,16,8192]{2,1,0:T(8,128)(2,1)}, bf16[4,16,8192]{2,1,0:T(8,128)(2,1)}, bf16[4,16,8192]{2,1,0:T(8,128)(2,1)}, bf16[4,16,81...) fusion(bf16[4,32,8192]{2,1,0:T(8,128)(2,1)S(1)} %bitcast.61, ...), kind=kLoop, calls=%fused_computation.35 | loop fusion | flops 3670016 | bytes 14680099 | tf_op jit(solution)/shard_map/jit(_where)/select_n | solution.py:14
  128.3 7.6 %convolution_bitcast_fusion = f32[4,98,8192]{2,1,0:T(8,128)} fusion(bf16[4,32,8192]{2,1,0:T(8,128)(2,1)S(1)} %bitcast.62, bf16[98,32]{1,0:T(8,128)(2,1)S(1)} %convert_element_type.85), kind=kOutput, calls=%fused_computation | convolution fusion | flops 205520896 | bytes 14948480 | tf_op jit(solution)/shard_map/rt,qtn->qrn/dot_general | solution.py:70
  135.9 105.2 %all-reduce.3.cloned.1.call-done = (bf16[4,16,8192]{2,1,0:T(8,128)(2,1)}, bf16[4,16,8192]{2,1,0:T(8,128)(2,1)}, bf16[4,16,8192]{2,1,0:T(8,128)(2,1)}, bf16[4,16,...) async-done(((bf16[4,16,8192]{2,1,0:T(8,128)(2,1)}, bf16[4,16,8192]{2,1,0:T(8,128)(2,1)}, ...) | async-done | bytes 7340048 | tf_op jit(solution)/shard_map/psum | solution.py:14
  241.1 1.7 convolution_bitcast_fusion.1
  244.6 1.7 convolution_bitcast_fusion.4
  246.3 1.7 convolution_bitcast_fusion.5
  248.1 1.7 convolution_bitcast_fusion.6
  249.8 1.8 convolution_bitcast_fusion.7
  251.6 15.3 %subtract_add_fusion = f32[4,7,8192]{2,1,0:T(8,128)} fusion(f32[4,98,8192]{2,1,0:T(8,128)} %convolution_bitcast_fusion, f32[4,14,8192]{2,1,0:T(8,128)S(1)} %convolution_bitcast_fusion.1, f32[4,14,8192]{2,1,0:T(8,128)S(1)} %convolution_bitcast_fusion.2, f32[4,14,8192]{2,1,0:T(8,128)S(1)} %convolution_bitcast_fusion.3, ...), kind=kLoop, calls=%fused_computation.27 | loop fusion | flops 6193152 | bytes 26607616 | tf_op jit(solution)/shard_map/add | solution.py:90
  266.9 15.6 %add_add_fusion = f32[4,7,8192]{2,1,0:T(8,128)} fusion(f32[4,98,8192]{2,1,0:T(8,128)} %convolution_bitcast_fusion, f32[4,14,8192]{2,1,0:T(8,128)S(1)} %convolution_bitcast_fusion.1, f32[4,14,8192]{2,1,0:T(8,128)S(1)} %convolution_bitcast_fusion.2, f32[4,14,8192]{2,1,0:T(8,128)S(1)} %convolution_bitcast_fusion.3, ...), kind=kLoop, calls=%fused_computation.28 | loop fusion | flops 6193152 | bytes 26607616 | tf_op jit(solution)/shard_map/add | solution.py:89
  282.6 1.8 reshape.339
  (61 shorter events, 12.5 us)
Async XLA Ops:
  7.9 9.5 %copy-start = (bf16[3,8,32,1024]{3,2,1,0:T(8,128)(2,1)S(1)}, bf16[3,8,32,1024]{3,2,1,0:T(8,128)(2,1)}, u32[]{:S(2)}) copy-start(bf16[3,8,32,1024]{3,2,1,0:T(8,128)(2,1)} %param.3) | copy-start | bytes 4718596
  8.1 5.3 %collective-permute-start = (bf16[2,8,2,1024]{3,1,2,0:T(8,128)(2,1)S(1)}, bf16[2,8,2,1024]{3,1,2,0:T(8,128)(2,1)S(1)}, u32[]{:S(2)}, u32[]{:S(2)}) collective-permute-start(bf16[2,8,2,1024]{3,1,2,0:T(8,128)(2,1)S(1)} %copy.47), channel_id=1, source_target_pairs={{0,16},{16,0},{1,17},{17,1},{2,18},{18,2},{3,19},{19,3},{4,20},{20... | collective-permute-start | bytes 196616 | tf_op jit(solution)/shard_map/ppermute | solution.py:24
  11.1 4.3 %collective-permute-start.1 = (bf16[2,8,2,1024]{3,1,2,0:T(8,128)(2,1)S(1)}, bf16[2,8,2,1024]{3,1,2,0:T(8,128)(2,1)S(1)}, u32[]{:S(2)}, u32[]{:S(2)}) collective-permute-start(bf16[2,8,2,1024]{3,1,2,0:T(8,128)(2,1)S(1)} %copy.48), channel_id=1, source_target_pairs={{16,0},{0,16},{17,1},{1,17},{18,2},{2,18},{19,3},{3,19},{20,4},{4,... | collective-permute-start | bytes 196616 | tf_op jit(solution)/shard_map/ppermute | solution.py:25
  15.6 7.9 %collective-permute-start.2 = (bf16[2,8,36,2]{3,1,2,0:T(8,128)(2,1)S(1)}, bf16[2,8,36,2]{3,1,2,0:T(8,128)(2,1)S(1)}, u32[]{:S(2)}, u32[]{:S(2)}) collective-permute-start(bf16[2,8,36,2]{3,1,2,0:T(8,128)(2,1)S(1)} %get-tuple-element.22), channel_id=1, source_target_pairs={{0,4},{4,8},{8,12},{12,0},{1,5},{5,9},{9,13},{13,1},{2,6},{6,10},{... | collective-permute-start | bytes 6920 | tf_op jit(solution)/shard_map/ppermute | solution.py:24
  15.7 7.8 %collective-permute-start.3 = (bf16[2,8,36,2]{3,1,2,0:T(8,128)(2,1)S(1)}, bf16[2,8,36,2]{3,1,2,0:T(8,128)(2,1)S(1)}, u32[]{:S(2)}, u32[]{:S(2)}) collective-permute-start(bf16[2,8,36,2]{3,1,2,0:T(8,128)(2,1)S(1)} %get-tuple-element.21), channel_id=1, source_target_pairs={{4,0},{8,4},{12,8},{0,12},{5,1},{9,5},{13,9},{1,13},{6,2},{10,6},{... | collective-permute-start | bytes 6920 | tf_op jit(solution)/shard_map/ppermute | solution.py:25
  32.3 5.7 %slice-start = ((s8[6291456]{0:T(1024)(128)(4,1)}), s8[4194304]{0:T(1024)(128)(4,1)S(1)}, s32[]{:S(2)}) async-start(s8[6291456]{0:T(1024)(128)(4,1)} %bitcast.64), calls=%async_computation.2 | async-start | bytes 8388608
  33.6 4.5 %slice-start.1 = ((s8[6291456]{0:T(1024)(128)(4,1)}), s8[2097152]{0:T(1024)(128)(4,1)S(1)}, s32[]{:S(2)}) async-start(s8[6291456]{0:T(1024)(128)(4,1)} %bitcast.64), calls=%async_computation.3 | async-start | bytes 4194304
  55.4 5.0 %copy-start.8 = (s32[7]{0:T(128)S(1)}, s32[7]{0:T(128)}, u32[]{:S(2)}) copy-start(s32[7]{0:T(128)} %param.4) | copy-start | bytes 88
  55.4 14.4 %copy-start.9 = (s32[7]{0:T(128)S(1)}, s32[7]{0:T(128)}, u32[]{:S(2)}) copy-start(s32[7]{0:T(128)} %param.5) | copy-start | bytes 88
  55.4 53.3 %all-to-all-start = ((bf16[4,2,131072]{2,1,0:T(2,128)(2,1)}), bf16[4,2,131072]{2,1,0:T(2,128)(2,1)S(1)}, u32[]{:S(2)}, u32[]{:S(2)}) async-start(bf16[4,2,131072]{2,1,0:T(2,128)(2,1)} %reshape.340), calls=%async_computation | async-start | bytes 4194304 | tf_op jit(solution)/shard_map/all_to_all | solution.py:68
  60.4 180.7 %all-reduce.3.cloned.1.call-start = ((), (), s32[]{:S(2)}) async-start(), calls=%async_computation.1 | async-start | bytes 14680064 | tf_op jit(solution)/shard_map/psum | solution.py:14
  241.1 1.7 copy-start.7
  242.9 1.2 copy-start.6
  243.3 1.3 copy-start.5
  244.5 1.8 copy-start.4
  246.3 1.8 copy-start.3
  248.1 1.7 copy-start.2
  282.6 1.8 copy-start.1
Sparse Core Ops, SparseCore 0:
  127.8 113.3 all-reduce.2
where the time goes:
time: 294 us; the launch traced here: 293 us
  waiting for transfers between devices  138 us (47%)
  other arithmetic  50.1 us (17%)
  local copies, waits for them, and re-layouts  46.7 us (16%)
  between operations  31 us (11%)
  matrix products  17.1 us (6%)
  starting transfers between devices  9.91 us (3%)
    psum x1, waiting for transfers between devices, from_root(): return lax.psum(jnp.where(mine, shard, jnp.zeros_like(shard)), axis)  105 us
    all_to_all x1, waiting for transfers between devices, shards(): lax.all_to_all(fields, 'ta', split_axis=3, concat_axis=1, tiled=True)  29.5 us
    unnamed x31, local copies, waits for them, and re-layouts  23.8 us
    add x1, other arithmetic, shards(): cospectrum + (remote_cos * cosine_part_here + remote_sin * local_sin)  15.6 us
    add x1, other arithmetic, shards(): quadrature_spectrum + (remote_cos * local_sin - remote_sin * cosine_part_...  15.3 us
    dot_general x7, matrix products, shards(): jnp.einsum('rt,qtn->qrn', window_rows, arrived, preferred_element_type=jn...  9.5 us
    all_to_all x1, local copies, waits for them, and re-layouts, shards(): lax.all_to_all(fields, 'ta', split_axis=3, concat_axis=1, tiled=True)  8.82 us
    dot_general x1, matrix products, shards(): jnp.einsum('rt,qtn->qrn', segment_rows, flat_series, preferred_element_ty...  7.59 us
  transfers between devices with their start and end apart: 6, of which 4 were waited for; matrix products, arithmetic and copies ran while one was open for 6% of the time, Pallas kernels for 0%

commit v1 on v0

--- a/solution.py
+++ b/solution.py
@@ -65,7 +65,15 @@
     fields = jnp.concatenate([velocity, vorticity[None]], axis=0)
     step_count_total = velocity.shape[1] * lax.axis_size("ta")
     segment_rows = dft_table(offsets, step_count_total)
-    series = lax.all_to_all(fields, "ta", split_axis=3, concat_axis=1, tiled=True)
+    ways, here = (lax.axis_size("ta"), lax.axis_index("ta"))
+    width_2 = fields.shape[3] // ways
+    turned = jnp.roll(fields, -here * width_2, axis=3)
+    got = [lax.slice_in_dim(turned, 0, width_2, axis=3)]
+    for far in range(1, ways):
+        sent = lax.slice_in_dim(turned, far * width_2, (far + 1) * width_2, axis=3)
+        got.append(lax.ppermute(sent, "ta", [(d, (d + far) % ways) for d in range(ways)]))
+    line = jnp.concatenate(got[::-1], axis=1)
+    series = jnp.roll(line, (here + 1) * got[0].shape[1], axis=1)
     flat_series = series.reshape(series.shape[0], series.shape[1], -1)
     power_spectra = jnp.einsum(
         "rt,qtn->qrn", segment_rows, flat_series, preferred_element_type=jnp.float32

time: 294 us -> 257 us (0.87)
  local copies, waits for them, and re-layouts: 46.7 us -> 17.8 us
  other arithmetic: 50.1 us -> 39.3 us
  waiting for transfers between devices: 138 us -> 142 us
    all_to_all x1 -> x0, waiting for transfers between devices: 29.5 us -> none  [shards(): lax.all_to_all(fields, 'ta', split_axis=3, concat_axis=1, tiled=True)]
    ppermute x0 -> x3, waiting for transfers between devices: none -> 26.5 us  [shards(): lax.ppermute(sent, 'ta', [(d, (d + far) % ways) for d in range(ways)])]
    unnamed x31 -> x27, local copies, waits for them, and re-layouts: 23.8 us -> 3.79 us
    all_to_all x1 -> x0, local copies, waits for them, and re-layouts: 8.82 us -> none  [shards(): lax.all_to_all(fields, 'ta', split_axis=3, concat_axis=1, tiled=True)]
    unnamed x2 -> x0, other arithmetic: 6.74 us -> none
    all_to_all x1 -> x0, starting transfers between devices: 5 us -> none  [shards(): lax.all_to_all(fields, 'ta', split_axis=3, concat_axis=1, tiled=True)]
    concatenate x3 -> x1, local copies, waits for them, and re-layouts: 6.07 us -> 1.46 us  [padded_2(): shard = jnp.concatenate([before, shard, after], axis=dim)]
    ppermute x0 -> x3, starting transfers between devices: none -> 4.58 us  [shards(): lax.ppermute(sent, 'ta', [(d, (d + far) % ways) for d in range(ways)])]
  transfers between devices with their start and end apart: 6 -> 8, of which waited for: 4 -> 6; matrix products, arithmetic and copies ran while one was open for 6% -> 4% of each run, Pallas kernels for 0% -> 0%
where the time goes in v1:
time: 257 us
  waiting for transfers between devices  142 us (55%)
  other arithmetic  39.3 us (15%)
  between operations  30.8 us (12%)
  local copies, waits for them, and re-layouts  17.8 us (7%)
  matrix products  17.3 us (7%)
  starting transfers between devices  9.48 us (4%)
    psum x1, waiting for transfers between devices, from_root(): return lax.psum(jnp.where(mine, shard, jnp.zeros_like(shard)), axis)  107 us
    ppermute x3, waiting for transfers between devices, shards(): lax.ppermute(sent, 'ta', [(d, (d + far) % ways) for d in range(ways)])  26.5 us
    add x1, other arithmetic, shards(): cospectrum + (remote_cos * cosine_part_here + remote_sin * local_sin)  15.5 us
    add x1, other arithmetic, shards(): quadrature_spectrum + (remote_cos * local_sin - remote_sin * cosine_part_...  15.3 us
    dot_general x7, matrix products, shards(): jnp.einsum('rt,qtn->qrn', window_rows, arrived, preferred_element_type=jn...  9.52 us
    dot_general x1, matrix products, shards(): jnp.einsum('rt,qtn->qrn', segment_rows, flat_series, preferred_element_ty...  7.8 us
  transfers between devices with their start and end apart: 8, of which 6 were waited for; matrix products, arithmetic and copies ran while one was open for 4% of the time, Pallas kernels for 0%

profile of v1, /device:TPU:0, one launch (start us, length us, event | category | flops | bytes accessed | tf_op | source)
XLA Modules:
  0.0 256.6 jit_solution(5635522639874455729)
XLA Ops:
  6.5 1.3 fusion.32
  7.9 3.0 %collective-permute-start.1 = (bf16[2,8,2,1024]{3,2,1,0:T(2,128)(2,1)S(1)}, bf16[2,8,2,1024]{3,2,1,0:T(2,128)(2,1)S(1)}, u32[]{:S(2)}, u32[]{:S(2)}) collective-permute-start(bf16[2,8,2,1024]{3,2,1,0:T(2,128)(2,1)S(1)} %get-tuple-element.27), channel_id=1, source_target_pairs={{16,0},{0,16},{17,1},{1,17},{18,2},{2,18},{19,3},{3,19},{20,4},{4,... | collective-permute-start | bytes 196616 | tf_op jit(solution)/shard_map/ppermute | solution.py:25
  11.1 2.3 collective-permute-done.1
  13.3 1.9 collective-permute-done
  16.2 1.7 collective-permute-start.3
  17.9 3.0 %collective-permute-done.2 = bf16[2,8,36,2]{3,2,1,0:T(8,128)(2,1)S(1)} collective-permute-done((bf16[2,8,36,2]{3,2,1,0:T(8,128)(2,1)S(1)}, bf16[2,8,36,2]{3,2,1,0:T(8,128)(2,1)S(1)}, u32[]{:S(2)}, u32[]{:S(2)}) %collective-permute-start.2) | collective-permute-done | bytes 2336 | tf_op jit(solution)/shard_map/ppermute | solution.py:24
  21.7 1.5 concatenate.21
  26.5 1.2 fusion.31
  27.7 3.6 %collective-permute-start.4 = (bf16[4,8,32,256]{3,2,1,0:T(8,128)(2,1)}, bf16[4,8,32,256]{3,2,1,0:T(8,128)(2,1)S(1)}, u32[]{:S(2)}, u32[]{:S(2)}) collective-permute-start(bf16[4,8,32,256]{3,2,1,0:T(8,128)(2,1)} %get-tuple-element.21), channel_id=1, source_target_pairs={{0,3},{1,0},{2,1},{3,2},{4,7},{5,4},{6,5},{7,6},{8,11},{9,8},{10,9... | collective-permute-start | bytes 1572872 | tf_op jit(solution)/shard_map/ppermute | solution.py:74
  50.8 26.5 %collective-permute-done.5 = bf16[4,8,32,256]{3,2,1,0:T(8,128)(2,1)S(1)} collective-permute-done((bf16[4,8,32,256]{3,2,1,0:T(8,128)(2,1)}, bf16[4,8,32,256]{3,2,1,0:T(8,128)(2,1)S(1)}, u32[]{:S(2)}, u32[]{:S(2)}) %collective-permute-start.5) | collective-permute-done | bytes 524320 | tf_op jit(solution)/shard_map/ppermute | solution.py:74
  79.8 1.5 constant_dynamic-slice_fusion
  81.3 2.9 %reshape.333 = bf16[4,32,8192]{2,1,0:T(8,128)(2,1)S(1)} reshape(bf16[4,32,32,256]{3,2,1,0:T(8,128)(2,1)} %constant_dynamic-slice_fusion) | data formatting | bytes 4194304 | tf_op jit(solution)/shard_map/reshape | solution.py:77
  84.2 4.5 %dynamic-slice_select_fusion.6 = (bf16[4,16,8192]{2,1,0:T(8,128)(2,1)}, bf16[4,16,8192]{2,1,0:T(8,128)(2,1)}, bf16[4,16,8192]{2,1,0:T(8,128)(2,1)}, bf16[4,16,81...) fusion(bf16[4,32,8192]{2,1,0:T(8,128)(2,1)S(1)} %reshape.333, ...), kind=kLoop, calls=%fused_computation.40 | loop fusion | flops 3670016 | bytes 14680099 | tf_op jit(solution)/shard_map/jit(_where)/select_n | solution.py:14
  89.4 7.8 %convolution_bitcast_fusion = f32[4,98,8192]{2,1,0:T(8,128)} fusion(bf16[4,32,8192]{2,1,0:T(8,128)(2,1)S(1)} %reshape.333, bf16[98,32]{1,0:T(8,128)(2,1)S(1)} %convert_element_type.85), kind=kOutput, calls=%fused_computation | convolution fusion | flops 205520896 | bytes 14948480 | tf_op jit(solution)/shard_map/rt,qtn->qrn/dot_general | solution.py:78
  97.2 107.4 %all-reduce.3.cloned.1.call-done = (bf16[4,16,8192]{2,1,0:T(8,128)(2,1)}, bf16[4,16,8192]{2,1,0:T(8,128)(2,1)}, bf16[4,16,8192]{2,1,0:T(8,128)(2,1)}, bf16[4,16,...) async-done(((bf16[4,16,8192]{2,1,0:T(8,128)(2,1)}, bf16[4,16,8192]{2,1,0:T(8,128)(2,1)}, ...) | async-done | bytes 7340048 | tf_op jit(solution)/shard_map/psum | solution.py:14
  204.6 1.7 convolution_bitcast_fusion.1
  208.1 1.8 convolution_bitcast_fusion.4
  209.8 1.7 convolution_bitcast_fusion.5
  211.6 1.7 convolution_bitcast_fusion.6
  213.3 1.8 convolution_bitcast_fusion.7
  215.0 15.3 %subtract_add_fusion = f32[4,7,8192]{2,1,0:T(8,128)} fusion(f32[4,98,8192]{2,1,0:T(8,128)} %convolution_bitcast_fusion, f32[4,14,8192]{2,1,0:T(8,128)S(1)} %convolution_bitcast_fusion.1, f32[4,14,8192]{2,1,0:T(8,128)S(1)} %convolution_bitcast_fusion.2, f32[4,14,8192]{2,1,0:T(8,128)S(1)} %convolution_bitcast_fusion.3, ...), kind=kLoop, calls=%fused_computation.32 | loop fusion | flops 6193152 | bytes 26607616 | tf_op jit(solution)/shard_map/add | solution.py:98
  230.4 15.5 %add_add_fusion = f32[4,7,8192]{2,1,0:T(8,128)} fusion(f32[4,98,8192]{2,1,0:T(8,128)} %convolution_bitcast_fusion, f32[4,14,8192]{2,1,0:T(8,128)S(1)} %convolution_bitcast_fusion.1, f32[4,14,8192]{2,1,0:T(8,128)S(1)} %convolution_bitcast_fusion.2, f32[4,14,8192]{2,1,0:T(8,128)S(1)} %convolution_bitcast_fusion.3, ...), kind=kLoop, calls=%fused_computation.33 | loop fusion | flops 6193152 | bytes 26607616 | tf_op jit(solution)/shard_map/add | solution.py:97
  245.9 1.8 reshape.338
  248.4 1.3 copy.9
  (61 shorter events, 12.9 us)
Async XLA Ops:
  6.5 198.0 %all-reduce.3.cloned.1.call-start = ((), (), s32[]{:S(2)}) async-start(), calls=%async_computation | async-start | bytes 14680064 | tf_op jit(solution)/shard_map/psum | solution.py:14
  7.9 5.4 %collective-permute-start.1 = (bf16[2,8,2,1024]{3,2,1,0:T(2,128)(2,1)S(1)}, bf16[2,8,2,1024]{3,2,1,0:T(2,128)(2,1)S(1)}, u32[]{:S(2)}, u32[]{:S(2)}) collective-permute-start(bf16[2,8,2,1024]{3,2,1,0:T(2,128)(2,1)S(1)} %get-tuple-element.27), channel_id=1, source_target_pairs={{16,0},{0,16},{17,1},{1,17},{18,2},{2,18},{19,3},{3,19},{20,4},{4,... | collective-permute-start | bytes 196616 | tf_op jit(solution)/shard_map/ppermute | solution.py:25
  11.0 4.3 %collective-permute-start = (bf16[2,8,2,1024]{3,2,1,0:T(2,128)(2,1)S(1)}, bf16[2,8,2,1024]{3,2,1,0:T(2,128)(2,1)S(1)}, u32[]{:S(2)}, u32[]{:S(2)}) collective-permute-start(bf16[2,8,2,1024]{3,2,1,0:T(2,128)(2,1)S(1)} %get-tuple-element.26), channel_id=1, source_target_pairs={{0,16},{16,0},{1,17},{17,1},{2,18},{18,2},{3,19},{19,3},{4,20},{20... | collective-permute-start | bytes 196616 | tf_op jit(solution)/shard_map/ppermute | solution.py:24
  16.1 4.8 %collective-permute-start.2 = (bf16[2,8,36,2]{3,2,1,0:T(8,128)(2,1)S(1)}, bf16[2,8,36,2]{3,2,1,0:T(8,128)(2,1)S(1)}, u32[]{:S(2)}, u32[]{:S(2)}) collective-permute-start(bf16[2,8,36,2]{3,2,1,0:T(8,128)(2,1)S(1)} %get-tuple-element.25), channel_id=1, source_target_pairs={{0,4},{4,8},{8,12},{12,0},{1,5},{5,9},{9,13},{13,1},{2,6},{6,10},{... | collective-permute-start | bytes 6920 | tf_op jit(solution)/shard_map/ppermute | solution.py:24
  16.2 5.5 %collective-permute-start.3 = (bf16[2,8,36,2]{3,2,1,0:T(8,128)(2,1)S(1)}, bf16[2,8,36,2]{3,2,1,0:T(8,128)(2,1)S(1)}, u32[]{:S(2)}, u32[]{:S(2)}) collective-permute-start(bf16[2,8,36,2]{3,2,1,0:T(8,128)(2,1)S(1)} %get-tuple-element.24), channel_id=1, source_target_pairs={{4,0},{8,4},{12,8},{0,12},{5,1},{9,5},{13,9},{1,13},{6,2},{10,6},{... | collective-permute-start | bytes 6920 | tf_op jit(solution)/shard_map/ppermute | solution.py:25
  23.9 1.4 copy-start
  26.5 5.8 %copy-start.8 = (s32[7]{0:T(128)S(1)}, s32[7]{0:T(128)}, u32[]{:S(2)}) copy-start(s32[7]{0:T(128)} %param.4) | copy-start | bytes 88
  26.5 14.9 %copy-start.9 = (s32[7]{0:T(128)S(1)}, s32[7]{0:T(128)}, u32[]{:S(2)}) copy-start(s32[7]{0:T(128)} %param.5) | copy-start | bytes 88
  27.7 23.0 %collective-permute-start.4 = (bf16[4,8,32,256]{3,2,1,0:T(8,128)(2,1)}, bf16[4,8,32,256]{3,2,1,0:T(8,128)(2,1)S(1)}, u32[]{:S(2)}, u32[]{:S(2)}) collective-permute-start(bf16[4,8,32,256]{3,2,1,0:T(8,128)(2,1)} %get-tuple-element.21), channel_id=1, source_target_pairs={{0,3},{1,0},{2,1},{3,2},{4,7},{5,4},{6,5},{7,6},{8,11},{9,8},{10,9... | collective-permute-start | bytes 1572872 | tf_op jit(solution)/shard_map/ppermute | solution.py:74
  31.3 46.0 %collective-permute-start.5 = (bf16[4,8,32,256]{3,2,1,0:T(8,128)(2,1)}, bf16[4,8,32,256]{3,2,1,0:T(8,128)(2,1)S(1)}, u32[]{:S(2)}, u32[]{:S(2)}) collective-permute-start(bf16[4,8,32,256]{3,2,1,0:T(8,128)(2,1)} %get-tuple-element.20), channel_id=1, source_target_pairs={{0,2},{1,3},{2,0},{3,1},{4,6},{5,7},{6,4},{7,5},{8,10},{9,11},{10,... | collective-permute-start | bytes 1572872 | tf_op jit(solution)/shard_map/ppermute | solution.py:74
  31.3 46.0 %collective-permute-start.6 = (bf16[4,8,32,256]{3,2,1,0:T(8,128)(2,1)}, bf16[4,8,32,256]{3,2,1,0:T(8,128)(2,1)}, u32[]{:S(2)}, u32[]{:S(2)}) collective-permute-start(bf16[4,8,32,256]{3,2,1,0:T(8,128)(2,1)} %get-tuple-element.19), channel_id=1, source_target_pairs={{0,1},{1,2},{2,3},{3,0},{4,5},{5,6},{6,7},{7,4},{8,9},{9,10},{10,1... | collective-permute-start | bytes 1572872 | tf_op jit(solution)/shard_map/ppermute | solution.py:74
  204.6 1.7 copy-start.7
  206.3 1.2 copy-start.6
  206.7 1.3 copy-start.5
  208.0 1.9 copy-start.4
  209.8 1.7 copy-start.3
  211.6 1.7 copy-start.2
  245.9 1.8 copy-start.1
Sparse Core Ops, SparseCore 0:
  88.8 115.6 all-reduce.2
